TPU v7x, 32 devices: a whole 2x2x4 slice. The times are simulated.
32 devices in a mesh: sec: 8 (over z, core), op: 4 (over y, x).
Axes of the slice: x: 2, y: 2, z: 4, core: 2. Of those that a mesh axis runs over, the one named last changes fastest.
Arguments:
- theta: float32 [16, 512, 512], P('sec', 'op'), may hold values from -6 to 6
- counts: int32 [16], P('sec'), may hold values from 256 to 512, as said below
- pair_source: int32 [32], P('sec'), may hold values from 0 to 1
- pair_target: int32 [32], P('sec'), may hold values from 0 to 15
- left_ops: float32 [128, 512, 512], P(('sec', 'op')), may hold values from -0.25 to 0.25
- right_ops: float32 [128, 512, 512], P(('sec', 'op')), may hold values from -0.25 to 0.25
Outputs:
- cheb_last: float32 [16, 512, 512], P('sec', 'op')
- cheb_prev: float32 [16, 512, 512], P('sec', 'op')
Inputs may be any that keep to these rules, and one draw needn't show every extreme that they name: `counts`: every sector has between 256 and 512 live states; some sector has exactly 512 and some exactly 256.
All inputs are finite; a program needn't handle non-finite values.
Results may differ from a plain program's by a relative error of at most 0.0001.
Values sent between devices are 32-bit elements; how exact they have to be, the bound alone decides.
No kernel may reach another device: no remote copies, remote signals or barrier semaphores. Data moves between devices by JAX's collectives and lax.ppermute only.
A program may use at most 64 MiB of HBM per device.

v0:
```python
import functools
import math

import jax
import jax.numpy as jnp
from jax import lax
from jax.experimental import pallas as pl
from jax.experimental.pallas import tpu as pltpu
from jax.sharding import PartitionSpec as P


STEPS = 3
CHUNKS = 2
CORES = 2
AXES = ("sec", "op")
MIB = 1 << 20

VMEM = pl.BlockSpec(memory_space=pltpu.VMEM)
SMEM = pl.BlockSpec(memory_space=pltpu.SMEM)


def params(mib):
    return pltpu.CompilerParams(vmem_limit_bytes=mib * MIB)


def partner_of(place, shift, count):
    if count & (count - 1) == 0:
        return place ^ shift
    return (place + shift) % count


def origin_of(place, shift, count):
    if count & (count - 1) == 0:
        return place ^ shift
    return (place + count - shift) % count


def split(value):
    high = value.astype(jnp.bfloat16)
    low = (value - high.astype(jnp.float32)).astype(jnp.bfloat16)
    return high, low


def three_pass(left_high, left_low, right_high, right_low):
    dot = functools.partial(jnp.dot, preferred_element_type=jnp.float32)
    return (
        dot(left_high, right_high)
        + dot(left_high, right_low)
        + dot(left_low, right_high)
    )


def prepare_kernel(left, right, left_high, left_low, right_high, right_low):
    left_high[0], left_low[0] = split(left[0])
    right_high[0], right_low[0] = split(right[0].T)


def prepare(left_ops, right_ops):
    pairs, order, _ = left_ops.shape
    spec = pl.BlockSpec((1, order, order), lambda p: (p, 0, 0))
    part = jax.ShapeDtypeStruct(left_ops.shape, jnp.bfloat16)
    return pl.pallas_call(
        prepare_kernel,
        grid=(pairs,),
        in_specs=[spec] * 2,
        out_specs=[spec] * 4,
        out_shape=[part] * 4,
        compiler_params=params(16),
        cost_estimate=pl.CostEstimate(
            flops=4 * pairs * order * order,
            bytes_accessed=16 * pairs * order * order,
            transcendentals=0,
        ),
        name="prepare",
    )(left_ops, right_ops)


def left_kernel(count, left_high, left_low, *refs):
    parts = refs[:count]
    out_high, out_low, high, low = refs[count:]
    place = lax.axis_index("op")
    rows = parts[0].shape[0]

    @pl.when(pl.program_id(0) == 0)
    def _():
        for shift in range(count):
            start = pl.multiple_of(origin_of(place, shift, count) * rows, rows)
            at = pl.ds(start, rows)
            high[at, :], low[at, :] = split(parts[shift][...])

    product = three_pass(left_high[0], left_low[0], high[...], low[...])
    out_high[0], out_low[0] = split(product)


def left_product(left, parts):
    pairs, order, _ = left[0].shape
    count = len(parts)
    rows, width = parts[0].shape
    op_spec = pl.BlockSpec((1, order, order), lambda p: (p, 0, 0))
    part_spec = pl.BlockSpec((rows, width), lambda p: (0, 0))
    out_spec = pl.BlockSpec((1, order, width), lambda p: (p, 0, 0))
    out = jax.ShapeDtypeStruct((pairs, order, width), jnp.bfloat16)
    return pl.pallas_call(
        functools.partial(left_kernel, count),
        grid=(pairs,),
        in_specs=[op_spec] * 2 + [part_spec] * count,
        out_specs=[out_spec] * 2,
        out_shape=[out] * 2,
        scratch_shapes=[pltpu.VMEM((order, width), jnp.bfloat16)] * 2,
        compiler_params=params(16),
        cost_estimate=pl.CostEstimate(
            flops=6 * pairs * order * order * width,
            bytes_accessed=4 * pairs * order * (order + width),
            transcendentals=0,
        ),
        name="left_product",
    )(*left, *parts)


def right_kernel(count, chunks, right_high, right_low, *refs):
    products = refs[: 2 * chunks]
    outs = refs[2 * chunks : 2 * chunks + count]
    total = refs[2 * chunks + count]
    place = lax.axis_index("op")
    pair = pl.program_id(0)
    width = products[0].shape[2]
    rows = outs[0].shape[0]
    term = None
    for chunk in range(chunks):
        at = pl.ds(chunk * width, width)
        part = three_pass(
            products[2 * chunk][0],
            products[2 * chunk + 1][0],
            right_high[0, at, :],
            right_low[0, at, :],
        )
        term = part if term is None else term + part

    @pl.when(pair == 0)
    def _():
        total[...] = term

    @pl.when(pair > 0)
    def _():
        total[...] += term

    @pl.when(pair == pl.num_programs(0) - 1)
    def _():
        for shift in range(count):
            start = pl.multiple_of(partner_of(place, shift, count) * rows, rows)
            outs[shift][...] = total[pl.ds(start, rows), :]


def right_product(right, products, chunk, count):
    pairs, order, width = products[0].shape
    rows = order // count
    op_spec = pl.BlockSpec((1, order, width), lambda p: (p, 0, chunk))
    product_spec = pl.BlockSpec((1, order, width), lambda p: (p, 0, 0))
    out_spec = pl.BlockSpec((rows, width), lambda p: (0, 0))
    chunks = len(products) // 2
    return pl.pallas_call(
        functools.partial(right_kernel, count, chunks),
        grid=(pairs,),
        in_specs=[op_spec] * 2 + [product_spec] * (2 * chunks),
        out_specs=[out_spec] * count,
        out_shape=[jax.ShapeDtypeStruct((rows, width), jnp.float32)] * count,
        scratch_shapes=[pltpu.VMEM((order, width), jnp.float32)],
        compiler_params=params(16),
        cost_estimate=pl.CostEstimate(
            flops=6 * pairs * order * order * width,
            bytes_accessed=4 * pairs * order * (order + width),
            transcendentals=0,
        ),
        name="right_product",
    )(*right, *products)


def scatter_kernel(count, sec_local, chips, own_target, other_target, *refs):
    own, other, outs, home = (
        refs[:count],
        refs[count],
        refs[count + 1 : count + chips],
        refs[count + chips],
    )
    sec, place = lax.axis_index("sec"), lax.axis_index("op")
    chip, core = lax.div(sec, CORES), lax.rem(sec, CORES)
    sign = 1 - 2 * core
    for out in (*outs, home):
        out[...] = jnp.zeros_like(out)
    for shift in range(count):
        block = origin_of(place, shift, count)
        for target, part in (
            (own_target[block], own[shift]),
            (other_target[block], other.at[shift]),
        ):
            target_sec = lax.div(target, sec_local)
            target_chip = lax.div(target_sec, CORES)
            slot = lax.rem(target, CORES * sec_local)
            distance = (target_chip - chip) * sign
            for step in range(1, chips):

                @pl.when(distance == step)
                def _(part=part, slot=slot, out=outs[step - 1]):
                    out[slot] += part[...]

            @pl.when(target_sec == sec)
            def _(part=part, target=target):
                home[lax.rem(target, sec_local)] += part[...]


def scatter(own_target, other_target, own, other, sec_local, chips):
    rows, width = own[0].shape
    count = len(own)
    far = jax.ShapeDtypeStruct((CORES * sec_local, rows, width), jnp.float32)
    home = jax.ShapeDtypeStruct((sec_local, rows, width), jnp.float32)
    *outs, home = pl.pallas_call(
        functools.partial(scatter_kernel, count, sec_local, chips),
        in_specs=[SMEM] * 2 + [VMEM] * (count + 1),
        out_specs=[VMEM] * chips,
        out_shape=[far] * (chips - 1) + [home],
        compiler_params=params(24),
        cost_estimate=pl.CostEstimate(
            flops=2 * count * rows * width,
            bytes_accessed=4 * rows * width * (4 * count + 4 * chips),
            transcendentals=0,
        ),
        name="scatter",
    )(own_target, other_target, *own, other)
    return outs, home


def gather_kernel(count, home, *refs):
    arrived, send, keep = refs[:count], refs[count], refs[count + 1]
    core = lax.rem(lax.axis_index("sec"), CORES)
    sec_local = home.shape[0]
    for sector in range(sec_local):
        mine = core * sec_local + sector
        theirs = (1 - core) * sec_local + sector
        first, second = arrived[0][theirs], home[sector] + arrived[0][mine]
        for part in arrived[1:]:
            first, second = first + part[theirs], second + part[mine]
        send[sector], keep[sector] = first, second


def gather(home, arrived):
    shape = jax.ShapeDtypeStruct(home.shape, jnp.float32)
    return pl.pallas_call(
        functools.partial(gather_kernel, len(arrived)),
        in_specs=[VMEM] * (1 + len(arrived)),
        out_specs=[VMEM] * 2,
        out_shape=[shape] * 2,
        compiler_params=params(16),
        cost_estimate=pl.CostEstimate(
            flops=home.size * 2 * len(arrived),
            bytes_accessed=home.size * 4 * (2 * len(arrived) + 3),
            transcendentals=0,
        ),
        name="gather",
    )(home, *arrived)


def finish_kernel(count, terms, scale, subtract, chunk, counts, source, *refs):
    summands, refs = refs[:terms], refs[terms:]
    if subtract:
        before, refs = refs[0], refs[1:]
    new, parts = refs[0], refs[1:]
    place = lax.axis_index("op")
    sec_local, rows, width = new.shape
    row = place * rows + lax.broadcasted_iota(jnp.int32, (rows, width), 0)
    column = chunk * width + lax.broadcasted_iota(jnp.int32, (rows, width), 1)
    for sector in range(sec_local):
        value = summands[0][sector]
        for summand in summands[1:]:
            value = value + summand[sector]
        live = (row < counts[sector]) & (column < counts[sector])
        value = jnp.where(live, scale * value, 0.0)
        if subtract:
            value = value - before[sector]
        new[sector] = value
    for shift in range(len(parts)):
        parts[shift][...] = new[source[partner_of(place, shift, count)]]


def finish(counts, source, summands, before, scale, chunk, chunks, send):
    sec_local, rows, width = summands[0].shape
    count = source.shape[0]
    whole = pl.BlockSpec((sec_local, rows, width), lambda i: (0, 0, 0))
    if chunks:
        width //= chunks
        whole = pl.BlockSpec((sec_local, rows, width), lambda i: (0, 0, chunk))
    spec = pl.BlockSpec((sec_local, rows, width), lambda i: (0, 0, 0))
    part_spec = pl.BlockSpec((rows, width), lambda i: (0, 0))
    operands = (*summands, *(() if before is None else (before,)))
    parts = count if send else 0
    return pl.pallas_call(
        functools.partial(
            finish_kernel,
            count,
            len(summands),
            scale,
            before is not None,
            chunk,
        ),
        grid=(1,),
        in_specs=[SMEM] * 2 + [whole if chunks else spec] * len(operands),
        out_specs=[spec] + [part_spec] * parts,
        out_shape=[jax.ShapeDtypeStruct((sec_local, rows, width), jnp.float32)]
        + [jax.ShapeDtypeStruct((rows, width), jnp.float32)] * parts,
        compiler_params=params(16),
        cost_estimate=pl.CostEstimate(
            flops=4 * sec_local * rows * width,
            bytes_accessed=4 * rows * width * (sec_local * 4 + parts),
            transcendentals=0,
        ),
        name="finish",
    )(counts, source, *operands)


def per_device(shape, theta, counts, source, target, left_ops, right_ops):
    secs, ops = shape["sec"], shape["op"]
    chips = secs // CORES
    sec_local, _, _ = theta.shape
    pairs = left_ops.shape[0]
    factor = 0.5 / math.sqrt(target.shape[0] * pairs / sec_local)

    def permute(value, where):
        pairs = []
        for sec in range(secs):
            for op in range(ops):
                to = where(sec, op)
                if to is not None:
                    pairs.append((sec * ops + op, to[0] * ops + to[1]))
        return lax.ppermute(value, AXES, pairs)

    def to_core(value):
        return permute(value, lambda sec, op: (sec ^ 1, op))

    def to_partners(parts):
        here = [parts[0]]
        for shift in range(1, ops):
            here.append(
                permute(
                    parts[shift],
                    lambda sec, op: (sec, partner_of(op, shift, ops)),
                )
            )
        return here

    def along(value, distance, levels):
        def where(sec, op):
            chip, core = sec // CORES, sec % CORES
            level = chip if core == 0 else chips - 1 - chip
            to = chip + (distance if core == 0 else -distance)
            if level in levels and level + distance < chips:
                return to * CORES + core, op
            return None

        return permute(value, where)

    other_target = to_core(target)

    def sums(pieces):
        own = to_partners(pieces)
        other = to_core(jnp.stack(own))
        outs, home = scatter(target, other_target, own, other, sec_local, chips)
        arrived = []
        every = set(range(chips))
        relay = None
        if chips > 2:
            relay = along(outs[1], 1, {0})
        for distance in range(2, chips):
            levels = every - {0} if distance == 2 else every
            if any(level + distance < chips for level in levels):
                arrived.append(along(outs[distance - 1], distance, levels))
        if chips > 1:
            last = outs[0] if relay is None else outs[0] + relay
            arrived.append(along(last, 1, every))
        if not arrived:
            return (home,)
        give, keep = gather(home, arrived)
        return keep, to_core(give)

    before = [None] * CHUNKS
    now, parts = [], []
    for chunk in range(CHUNKS):
        new, *send = finish(
            counts, source, (theta,), None, 1.0, chunk, CHUNKS, True
        )
        now.append(new)
        parts.append(to_partners(send))
    prepared = prepare(left_ops, right_ops)
    left, right = prepared[:2], prepared[2:]
    products = []
    for chunk in range(CHUNKS):
        products.extend(left_product(left, parts[chunk]))
    for step in range(STEPS):
        parts, after = [], []
        for chunk in range(CHUNKS):
            pieces = right_product(right, products, chunk, ops)
            terms = sums(pieces)
            new, *send = finish(
                counts,
                source,
                terms,
                before[chunk],
                factor if step == 0 else 2.0 * factor,
                chunk,
                0,
                step < STEPS - 1,
            )
            after.append(new)
            if send:
                parts.append(to_partners(send))
        before, now, products = now, after, []
        for chunk in range(len(parts)):
            products.extend(left_product(left, parts[chunk]))
    return jnp.concatenate(now, axis=2), jnp.concatenate(before, axis=2)


def solution(mesh):
    in_specs = (
        P("sec", "op", None),
        P("sec"),
        P("sec"),
        P("sec"),
        P(("sec", "op"), None, None),
        P(("sec", "op"), None, None),
    )
    out_specs = (P("sec", "op", None), P("sec", "op", None))
    return jax.shard_map(
        functools.partial(per_device, dict(mesh.shape)),
        mesh=mesh,
        in_specs=in_specs,
        out_specs=out_specs,
        check_vma=False,
    )
```

profile of v0, /device:TPU:0, one launch (start us, length us, event | category | flops | bytes accessed | tf_op | source)
XLA Modules:
  0.0 254.4 jit_solution(16893474311630549382)
XLA Ops:
  3.6 3.0 %collective-permute-start.4 = (f32[128,256]{1,0:T(8,128)S(1)}, f32[128,256]{1,0:T(8,128)S(1)}, u32[]{:S(2)}, u32[]{:S(2)}) collective-permute-start(f32[128,256]{1,0:T(8,128)S(1)} %get-tuple-element.119), channel_id=1, source_target_pairs={{0,1},{1,0},{2,3},{3,2},{4,5},{5,4},{6,7},{7,6},{8,9},{9,8},{10,11... | collective-permute-start | bytes 393224 | tf_op jit(solution)/shard_map/ppermute | solution.py:333
  21.5 3.4 %collective-permute-done.3.refs_3_ = f32[128,256]{1,0:T(8,128)S(1)} collective-permute-done((f32[128,256]{1,0:T(8,128)S(1)}, f32[128,256]{1,0:T(8,128)S(1)}, u32[]{:S(2)}, u32[]{:S(2)}) %collective-permute-start.3) | collective-permute-done | bytes 131104 | tf_op jit(solution)/shard_map/ppermute | solution.py:333
  46.3 3.5 %collective-permute-start.25 = (f32[4,128,256]{2,1,0:T(8,128)S(1)}, f32[4,128,256]{2,1,0:T(8,128)S(1)}, u32[]{:S(2)}, u32[]{:S(2)}) collective-permute-start(f32[4,128,256]{2,1,0:T(8,128)S(1)} %get-tuple-element.145), channel_id=1, source_target_pairs={{0,8},{1,9},{2,10},{3,11},{28,20},{29,21},{30,22},{31,23}} | collective-permute-start | bytes 1572872 | tf_op jit(solution)/shard_map/ppermute | solution.py:333
  56.5 4.4 %collective-permute-start.26 = (f32[4,128,256]{2,1,0:T(8,128)S(1)}, f32[4,128,256]{2,1,0:T(8,128)S(1)}, u32[]{:S(2)}, u32[]{:S(2)}) collective-permute-start(f32[4,128,256]{2,1,0:T(8,128)S(1)} %add.19), channel_id=1, source_target_pairs={{0,8},{1,9},{2,10},{3,11},{8,16},{9,17},{10,18},{11,19},{12,4},{13... | collective-permute-start | bytes 1572872 | tf_op jit(solution)/shard_map/ppermute | solution.py:333
  63.5 4.2 %collective-permute-done.24.refs_1_ = f32[4,128,256]{2,1,0:T(8,128)S(1)} collective-permute-done((f32[4,128,256]{2,1,0:T(8,128)S(1)}, f32[4,128,256]{2,1,0:T(8,128)S(1)}, u32[]{:S(2)}, u32[]{:S(2)}) %collective-permute-start.24) | collective-permute-done | bytes 524320 | tf_op jit(solution)/shard_map/ppermute | solution.py:333
  69.0 4.3 %collective-permute-done.26.refs_2_ = f32[4,128,256]{2,1,0:T(8,128)S(1)} collective-permute-done((f32[4,128,256]{2,1,0:T(8,128)S(1)}, f32[4,128,256]{2,1,0:T(8,128)S(1)}, u32[]{:S(2)}, u32[]{:S(2)}) %collective-permute-start.26) | collective-permute-done | bytes 524320 | tf_op jit(solution)/shard_map/ppermute | solution.py:333
  73.5 5.5 %collective-permute-done.12.refs_1_ = f32[4,128,256]{2,1,0:T(8,128)S(1)} collective-permute-done((f32[4,128,256]{2,1,0:T(8,128)S(1)}, f32[4,128,256]{2,1,0:T(8,128)S(1)}, u32[]{:S(2)}, u32[]{:S(2)}) %collective-permute-start.12) | collective-permute-done | bytes 524320 | tf_op jit(solution)/shard_map/ppermute | solution.py:333
  79.0 5.6 %collective-permute-done.14.refs_2_ = f32[4,128,256]{2,1,0:T(8,128)S(1)} collective-permute-done((f32[4,128,256]{2,1,0:T(8,128)S(1)}, f32[4,128,256]{2,1,0:T(8,128)S(1)}, u32[]{:S(2)}, u32[]{:S(2)}) %collective-permute-start.14) | collective-permute-done | bytes 524320 | tf_op jit(solution)/shard_map/ppermute | solution.py:333
  84.8 5.1 %collective-permute-start.15 = (f32[2,128,256]{2,1,0:T(8,128)S(1)}, f32[2,128,256]{2,1,0:T(8,128)S(1)}, u32[]{:S(2)}, u32[]{:S(2)}) collective-permute-start(f32[2,128,256]{2,1,0:T(8,128)S(1)} %get-tuple-element.133), channel_id=1, source_target_pairs={{0,4},{1,5},{2,6},{3,7},{4,0},{5,1},{6,2},{7,3},{8,12},{9,13},{10,... | collective-permute-start | bytes 786440 | tf_op jit(solution)/shard_map/ppermute | solution.py:333
  126.4 3.5 %collective-permute-start.49 = (f32[4,128,256]{2,1,0:T(8,128)S(1)}, f32[4,128,256]{2,1,0:T(8,128)S(1)}, u32[]{:S(2)}, u32[]{:S(2)}) collective-permute-start(f32[4,128,256]{2,1,0:T(8,128)S(1)} %get-tuple-element.178), channel_id=1, source_target_pairs={{0,8},{1,9},{2,10},{3,11},{28,20},{29,21},{30,22},{31,23}} | collective-permute-start | bytes 1572872 | tf_op jit(solution)/shard_map/ppermute | solution.py:333
  132.4 3.0 %collective-permute-start.48 = (f32[4,128,256]{2,1,0:T(8,128)S(1)}, f32[4,128,256]{2,1,0:T(8,128)S(1)}, u32[]{:S(2)}, u32[]{:S(2)}) collective-permute-start(f32[4,128,256]{2,1,0:T(8,128)S(1)} %get-tuple-element.179), channel_id=1, source_target_pairs={{0,24},{1,25},{2,26},{3,27},{28,4},{29,5},{30,6},{31,7}} | collective-permute-start | bytes 1572872 | tf_op jit(solution)/shard_map/ppermute | solution.py:333
  136.6 4.4 %collective-permute-start.50 = (f32[4,128,256]{2,1,0:T(8,128)S(1)}, f32[4,128,256]{2,1,0:T(8,128)S(1)}, u32[]{:S(2)}, u32[]{:S(2)}) collective-permute-start(f32[4,128,256]{2,1,0:T(8,128)S(1)} %add.21), channel_id=1, source_target_pairs={{0,8},{1,9},{2,10},{3,11},{8,16},{9,17},{10,18},{11,19},{12,4},{13... | collective-permute-start | bytes 1572872 | tf_op jit(solution)/shard_map/ppermute | solution.py:333
  143.6 4.3 %collective-permute-done.48.refs_1_ = f32[4,128,256]{2,1,0:T(8,128)S(1)} collective-permute-done((f32[4,128,256]{2,1,0:T(8,128)S(1)}, f32[4,128,256]{2,1,0:T(8,128)S(1)}, u32[]{:S(2)}, u32[]{:S(2)}) %collective-permute-start.48) | collective-permute-done | bytes 524320 | tf_op jit(solution)/shard_map/ppermute | solution.py:333
  149.2 4.3 %collective-permute-done.50.refs_2_ = f32[4,128,256]{2,1,0:T(8,128)S(1)} collective-permute-done((f32[4,128,256]{2,1,0:T(8,128)S(1)}, f32[4,128,256]{2,1,0:T(8,128)S(1)}, u32[]{:S(2)}, u32[]{:S(2)}) %collective-permute-start.50) | collective-permute-done | bytes 524320 | tf_op jit(solution)/shard_map/ppermute | solution.py:333
  153.7 5.4 %collective-permute-done.36.refs_1_ = f32[4,128,256]{2,1,0:T(8,128)S(1)} collective-permute-done((f32[4,128,256]{2,1,0:T(8,128)S(1)}, f32[4,128,256]{2,1,0:T(8,128)S(1)}, u32[]{:S(2)}, u32[]{:S(2)}) %collective-permute-start.36) | collective-permute-done | bytes 524320 | tf_op jit(solution)/shard_map/ppermute | solution.py:333
  159.1 5.6 %collective-permute-done.38.refs_2_ = f32[4,128,256]{2,1,0:T(8,128)S(1)} collective-permute-done((f32[4,128,256]{2,1,0:T(8,128)S(1)}, f32[4,128,256]{2,1,0:T(8,128)S(1)}, u32[]{:S(2)}, u32[]{:S(2)}) %collective-permute-start.38) | collective-permute-done | bytes 524320 | tf_op jit(solution)/shard_map/ppermute | solution.py:333
  164.9 6.4 %collective-permute-start.39 = (f32[2,128,256]{2,1,0:T(8,128)S(1)}, f32[2,128,256]{2,1,0:T(8,128)S(1)}, u32[]{:S(2)}, u32[]{:S(2)}) collective-permute-start(f32[2,128,256]{2,1,0:T(8,128)S(1)} %get-tuple-element.165), channel_id=1, source_target_pairs={{0,4},{1,5},{2,6},{3,7},{4,0},{5,1},{6,2},{7,3},{8,12},{9,13},{10,... | collective-permute-start | bytes 786440 | tf_op jit(solution)/shard_map/ppermute | solution.py:333
  207.5 3.4 %collective-permute-start.61 = (f32[4,128,256]{2,1,0:T(8,128)S(1)}, f32[4,128,256]{2,1,0:T(8,128)S(1)}, u32[]{:S(2)}, u32[]{:S(2)}) collective-permute-start(f32[4,128,256]{2,1,0:T(8,128)S(1)} %get-tuple-element.195), channel_id=1, source_target_pairs={{0,8},{1,9},{2,10},{3,11},{28,20},{29,21},{30,22},{31,23}} | collective-permute-start | bytes 1572872 | tf_op jit(solution)/shard_map/ppermute | solution.py:333
  213.2 3.0 %collective-permute-start.60 = (f32[4,128,256]{2,1,0:T(8,128)S(1)}, f32[4,128,256]{2,1,0:T(8,128)S(1)}, u32[]{:S(2)}, u32[]{:S(2)}) collective-permute-start(f32[4,128,256]{2,1,0:T(8,128)S(1)} %get-tuple-element.196), channel_id=1, source_target_pairs={{0,24},{1,25},{2,26},{3,27},{28,4},{29,5},{30,6},{31,7}} | collective-permute-start | bytes 1572872 | tf_op jit(solution)/shard_map/ppermute | solution.py:333
  217.7 4.3 %collective-permute-start.62 = (f32[4,128,256]{2,1,0:T(8,128)S(1)}, f32[4,128,256]{2,1,0:T(8,128)S(1)}, u32[]{:S(2)}, u32[]{:S(2)}) collective-permute-start(f32[4,128,256]{2,1,0:T(8,128)S(1)} %add.22), channel_id=1, source_target_pairs={{0,8},{1,9},{2,10},{3,11},{8,16},{9,17},{10,18},{11,19},{12,4},{13... | collective-permute-start | bytes 1572872 | tf_op jit(solution)/shard_map/ppermute | solution.py:333
  224.5 4.3 %collective-permute-done.60.refs_1_ = f32[4,128,256]{2,1,0:T(8,128)S(1)} collective-permute-done((f32[4,128,256]{2,1,0:T(8,128)S(1)}, f32[4,128,256]{2,1,0:T(8,128)S(1)}, u32[]{:S(2)}, u32[]{:S(2)}) %collective-permute-start.60) | collective-permute-done | bytes 524320 | tf_op jit(solution)/shard_map/ppermute | solution.py:333
  230.1 4.3 %collective-permute-done.62.refs_2_ = f32[4,128,256]{2,1,0:T(8,128)S(1)} collective-permute-done((f32[4,128,256]{2,1,0:T(8,128)S(1)}, f32[4,128,256]{2,1,0:T(8,128)S(1)}, u32[]{:S(2)}, u32[]{:S(2)}) %collective-permute-start.62) | collective-permute-done | bytes 524320 | tf_op jit(solution)/shard_map/ppermute | solution.py:333
  234.5 11.3 %collective-permute-start.63 = (f32[2,128,256]{2,1,0:T(8,128)S(1)}, f32[2,128,256]{2,1,0:T(8,128)S(1)}, u32[]{:S(2)}, u32[]{:S(2)}) collective-permute-start(f32[2,128,256]{2,1,0:T(8,128)S(1)} %get-tuple-element.199), channel_id=1, source_target_pairs={{0,4},{1,5},{2,6},{3,7},{4,0},{5,1},{6,2},{7,3},{8,12},{9,13},{10,... | collective-permute-start | bytes 786440 | tf_op jit(solution)/shard_map/ppermute | solution.py:333
  246.0 5.5 %collective-permute-start.72 = (f32[2,128,256]{2,1,0:T(8,128)S(1)}, f32[2,128,256]{2,1,0:T(8,128)S(1)}, u32[]{:S(2)}, u32[]{:S(2)}) collective-permute-start(f32[2,128,256]{2,1,0:T(8,128)S(1)} %get-tuple-element.210), channel_id=1, source_target_pairs={{0,4},{1,5},{2,6},{3,7},{4,0},{5,1},{6,2},{7,3},{8,12},{9,13},{10,... | collective-permute-start | bytes 786440 | tf_op jit(solution)/shard_map/ppermute | solution.py:333
  (185 shorter events, 141.0 us)
Async XLA Ops:
  3.6 15.3 %collective-permute-start.4 = (f32[128,256]{1,0:T(8,128)S(1)}, f32[128,256]{1,0:T(8,128)S(1)}, u32[]{:S(2)}, u32[]{:S(2)}) collective-permute-start(f32[128,256]{1,0:T(8,128)S(1)} %get-tuple-element.119), channel_id=1, source_target_pairs={{0,1},{1,0},{2,3},{3,2},{4,5},{5,4},{6,7},{7,6},{8,9},{9,8},{10,11... | collective-permute-start | bytes 393224 | tf_op jit(solution)/shard_map/ppermute | solution.py:333
  6.6 12.4 %collective-permute-start.5 = (f32[128,256]{1,0:T(8,128)S(1)}, f32[128,256]{1,0:T(8,128)S(1)}, u32[]{:S(2)}, u32[]{:S(2)}) collective-permute-start(f32[128,256]{1,0:T(8,128)S(1)} %get-tuple-element.120), channel_id=1, source_target_pairs={{0,2},{1,3},{2,0},{3,1},{4,6},{5,7},{6,4},{7,5},{8,10},{9,11},{10,... | collective-permute-start | bytes 393224 | tf_op jit(solution)/shard_map/ppermute | solution.py:333
  8.8 12.7 %collective-permute-start.1 = (f32[128,256]{1,0:T(8,128)S(1)}, f32[128,256]{1,0:T(8,128)S(1)}, u32[]{:S(2)}, u32[]{:S(2)}) collective-permute-start(f32[128,256]{1,0:T(8,128)S(1)} %get-tuple-element.113), channel_id=1, source_target_pairs={{0,1},{1,0},{2,3},{3,2},{4,5},{5,4},{6,7},{7,6},{8,9},{9,8},{10,11... | collective-permute-start | bytes 393224 | tf_op jit(solution)/shard_map/ppermute | solution.py:333
  52.1 15.6 %collective-permute-start.24 = (f32[4,128,256]{2,1,0:T(8,128)S(1)}, f32[4,128,256]{2,1,0:T(8,128)S(1)}, u32[]{:S(2)}, u32[]{:S(2)}) collective-permute-start(f32[4,128,256]{2,1,0:T(8,128)S(1)} %get-tuple-element.146), channel_id=1, source_target_pairs={{0,24},{1,25},{2,26},{3,27},{28,4},{29,5},{30,6},{31,7}} | collective-permute-start | bytes 1572872 | tf_op jit(solution)/shard_map/ppermute | solution.py:333
  54.1 14.9 %collective-permute-start.23 = (f32[4,128,256]{2,1,0:T(8,128)S(1)}, f32[4,128,256]{2,1,0:T(8,128)S(1)}, u32[]{:S(2)}, u32[]{:S(2)}) collective-permute-start(f32[4,128,256]{2,1,0:T(8,128)S(1)} %get-tuple-element.145), channel_id=1, source_target_pairs={{8,24},{9,25},{10,26},{11,27},{20,4},{21,5},{22,6},{23,7}} | collective-permute-start | bytes 1572872 | tf_op jit(solution)/shard_map/ppermute | solution.py:333
  56.5 16.8 %collective-permute-start.26 = (f32[4,128,256]{2,1,0:T(8,128)S(1)}, f32[4,128,256]{2,1,0:T(8,128)S(1)}, u32[]{:S(2)}, u32[]{:S(2)}) collective-permute-start(f32[4,128,256]{2,1,0:T(8,128)S(1)} %add.19), channel_id=1, source_target_pairs={{0,8},{1,9},{2,10},{3,11},{8,16},{9,17},{10,18},{11,19},{12,4},{13... | collective-permute-start | bytes 1572872 | tf_op jit(solution)/shard_map/ppermute | solution.py:333
  60.9 18.1 %collective-permute-start.11 = (f32[4,128,256]{2,1,0:T(8,128)S(1)}, f32[4,128,256]{2,1,0:T(8,128)S(1)}, u32[]{:S(2)}, u32[]{:S(2)}) collective-permute-start(f32[4,128,256]{2,1,0:T(8,128)S(1)} %get-tuple-element.129), channel_id=1, source_target_pairs={{8,24},{9,25},{10,26},{11,27},{20,4},{21,5},{22,6},{23,7}} | collective-permute-start | bytes 1572872 | tf_op jit(solution)/shard_map/ppermute | solution.py:333
  62.0 17.0 %collective-permute-start.12 = (f32[4,128,256]{2,1,0:T(8,128)S(1)}, f32[4,128,256]{2,1,0:T(8,128)S(1)}, u32[]{:S(2)}, u32[]{:S(2)}) collective-permute-start(f32[4,128,256]{2,1,0:T(8,128)S(1)} %get-tuple-element.130), channel_id=1, source_target_pairs={{0,24},{1,25},{2,26},{3,27},{28,4},{29,5},{30,6},{31,7}} | collective-permute-start | bytes 1572872 | tf_op jit(solution)/shard_map/ppermute | solution.py:333
  67.7 16.9 %collective-permute-start.14 = (f32[4,128,256]{2,1,0:T(8,128)S(1)}, f32[4,128,256]{2,1,0:T(8,128)S(1)}, u32[]{:S(2)}, u32[]{:S(2)}) collective-permute-start(f32[4,128,256]{2,1,0:T(8,128)S(1)} %add.18), channel_id=1, source_target_pairs={{0,8},{1,9},{2,10},{3,11},{8,16},{9,17},{10,18},{11,19},{12,4},{13... | collective-permute-start | bytes 1572872 | tf_op jit(solution)/shard_map/ppermute | solution.py:333
  73.5 16.4 %collective-permute-start.27 = (f32[2,128,256]{2,1,0:T(8,128)S(1)}, f32[2,128,256]{2,1,0:T(8,128)S(1)}, u32[]{:S(2)}, u32[]{:S(2)}) collective-permute-start(f32[2,128,256]{2,1,0:T(8,128)S(1)} %get-tuple-element.149), channel_id=1, source_target_pairs={{0,4},{1,5},{2,6},{3,7},{4,0},{5,1},{6,2},{7,3},{8,12},{9,13},{10,... | collective-permute-start | bytes 786440 | tf_op jit(solution)/shard_map/ppermute | solution.py:333
  132.4 15.4 %collective-permute-start.48 = (f32[4,128,256]{2,1,0:T(8,128)S(1)}, f32[4,128,256]{2,1,0:T(8,128)S(1)}, u32[]{:S(2)}, u32[]{:S(2)}) collective-permute-start(f32[4,128,256]{2,1,0:T(8,128)S(1)} %get-tuple-element.179), channel_id=1, source_target_pairs={{0,24},{1,25},{2,26},{3,27},{28,4},{29,5},{30,6},{31,7}} | collective-permute-start | bytes 1572872 | tf_op jit(solution)/shard_map/ppermute | solution.py:333
  135.4 13.7 %collective-permute-start.47 = (f32[4,128,256]{2,1,0:T(8,128)S(1)}, f32[4,128,256]{2,1,0:T(8,128)S(1)}, u32[]{:S(2)}, u32[]{:S(2)}) collective-permute-start(f32[4,128,256]{2,1,0:T(8,128)S(1)} %get-tuple-element.178), channel_id=1, source_target_pairs={{8,24},{9,25},{10,26},{11,27},{20,4},{21,5},{22,6},{23,7}} | collective-permute-start | bytes 1572872 | tf_op jit(solution)/shard_map/ppermute | solution.py:333
  136.6 16.8 %collective-permute-start.50 = (f32[4,128,256]{2,1,0:T(8,128)S(1)}, f32[4,128,256]{2,1,0:T(8,128)S(1)}, u32[]{:S(2)}, u32[]{:S(2)}) collective-permute-start(f32[4,128,256]{2,1,0:T(8,128)S(1)} %add.21), channel_id=1, source_target_pairs={{0,8},{1,9},{2,10},{3,11},{8,16},{9,17},{10,18},{11,19},{12,4},{13... | collective-permute-start | bytes 1572872 | tf_op jit(solution)/shard_map/ppermute | solution.py:333
  141.1 18.1 %collective-permute-start.35 = (f32[4,128,256]{2,1,0:T(8,128)S(1)}, f32[4,128,256]{2,1,0:T(8,128)S(1)}, u32[]{:S(2)}, u32[]{:S(2)}) collective-permute-start(f32[4,128,256]{2,1,0:T(8,128)S(1)} %get-tuple-element.161), channel_id=1, source_target_pairs={{8,24},{9,25},{10,26},{11,27},{20,4},{21,5},{22,6},{23,7}} | collective-permute-start | bytes 1572872 | tf_op jit(solution)/shard_map/ppermute | solution.py:333
  142.2 16.9 %collective-permute-start.36 = (f32[4,128,256]{2,1,0:T(8,128)S(1)}, f32[4,128,256]{2,1,0:T(8,128)S(1)}, u32[]{:S(2)}, u32[]{:S(2)}) collective-permute-start(f32[4,128,256]{2,1,0:T(8,128)S(1)} %get-tuple-element.162), channel_id=1, source_target_pairs={{0,24},{1,25},{2,26},{3,27},{28,4},{29,5},{30,6},{31,7}} | collective-permute-start | bytes 1572872 | tf_op jit(solution)/shard_map/ppermute | solution.py:333
  147.8 16.9 %collective-permute-start.38 = (f32[4,128,256]{2,1,0:T(8,128)S(1)}, f32[4,128,256]{2,1,0:T(8,128)S(1)}, u32[]{:S(2)}, u32[]{:S(2)}) collective-permute-start(f32[4,128,256]{2,1,0:T(8,128)S(1)} %add.20), channel_id=1, source_target_pairs={{0,8},{1,9},{2,10},{3,11},{8,16},{9,17},{10,18},{11,19},{12,4},{13... | collective-permute-start | bytes 1572872 | tf_op jit(solution)/shard_map/ppermute | solution.py:333
  153.6 17.6 %collective-permute-start.51 = (f32[2,128,256]{2,1,0:T(8,128)S(1)}, f32[2,128,256]{2,1,0:T(8,128)S(1)}, u32[]{:S(2)}, u32[]{:S(2)}) collective-permute-start(f32[2,128,256]{2,1,0:T(8,128)S(1)} %get-tuple-element.182), channel_id=1, source_target_pairs={{0,4},{1,5},{2,6},{3,7},{4,0},{5,1},{6,2},{7,3},{8,12},{9,13},{10,... | collective-permute-start | bytes 786440 | tf_op jit(solution)/shard_map/ppermute | solution.py:333
  213.2 15.6 %collective-permute-start.60 = (f32[4,128,256]{2,1,0:T(8,128)S(1)}, f32[4,128,256]{2,1,0:T(8,128)S(1)}, u32[]{:S(2)}, u32[]{:S(2)}) collective-permute-start(f32[4,128,256]{2,1,0:T(8,128)S(1)} %get-tuple-element.196), channel_id=1, source_target_pairs={{0,24},{1,25},{2,26},{3,27},{28,4},{29,5},{30,6},{31,7}} | collective-permute-start | bytes 1572872 | tf_op jit(solution)/shard_map/ppermute | solution.py:333
  216.2 13.9 %collective-permute-start.59 = (f32[4,128,256]{2,1,0:T(8,128)S(1)}, f32[4,128,256]{2,1,0:T(8,128)S(1)}, u32[]{:S(2)}, u32[]{:S(2)}) collective-permute-start(f32[4,128,256]{2,1,0:T(8,128)S(1)} %get-tuple-element.195), channel_id=1, source_target_pairs={{8,24},{9,25},{10,26},{11,27},{20,4},{21,5},{22,6},{23,7}} | collective-permute-start | bytes 1572872 | tf_op jit(solution)/shard_map/ppermute | solution.py:333
  216.9 29.0 %collective-permute-start.68 = (f32[4,128,256]{2,1,0:T(8,128)S(1)}, f32[4,128,256]{2,1,0:T(8,128)S(1)}, u32[]{:S(2)}, u32[]{:S(2)}) collective-permute-start(f32[4,128,256]{2,1,0:T(8,128)S(1)} %get-tuple-element.206), channel_id=1, source_target_pairs={{8,24},{9,25},{10,26},{11,27},{20,4},{21,5},{22,6},{23,7}} | collective-permute-start | bytes 1572872 | tf_op jit(solution)/shard_map/ppermute | solution.py:333
  217.7 16.7 %collective-permute-start.62 = (f32[4,128,256]{2,1,0:T(8,128)S(1)}, f32[4,128,256]{2,1,0:T(8,128)S(1)}, u32[]{:S(2)}, u32[]{:S(2)}) collective-permute-start(f32[4,128,256]{2,1,0:T(8,128)S(1)} %add.22), channel_id=1, source_target_pairs={{0,8},{1,9},{2,10},{3,11},{8,16},{9,17},{10,18},{11,19},{12,4},{13... | collective-permute-start | bytes 1572872 | tf_op jit(solution)/shard_map/ppermute | solution.py:333
  223.1 22.7 %collective-permute-start.69 = (f32[4,128,256]{2,1,0:T(8,128)S(1)}, f32[4,128,256]{2,1,0:T(8,128)S(1)}, u32[]{:S(2)}, u32[]{:S(2)}) collective-permute-start(f32[4,128,256]{2,1,0:T(8,128)S(1)} %get-tuple-element.207), channel_id=1, source_target_pairs={{0,24},{1,25},{2,26},{3,27},{28,4},{29,5},{30,6},{31,7}} | collective-permute-start | bytes 1572872 | tf_op jit(solution)/shard_map/ppermute | solution.py:333
  228.8 17.1 %collective-permute-start.71 = (f32[4,128,256]{2,1,0:T(8,128)S(1)}, f32[4,128,256]{2,1,0:T(8,128)S(1)}, u32[]{:S(2)}, u32[]{:S(2)}) collective-permute-start(f32[4,128,256]{2,1,0:T(8,128)S(1)} %add.23), channel_id=1, source_target_pairs={{0,8},{1,9},{2,10},{3,11},{8,16},{9,17},{10,18},{11,19},{12,4},{13... | collective-permute-start | bytes 1572872 | tf_op jit(solution)/shard_map/ppermute | solution.py:333
  234.5 17.8 %collective-permute-start.63 = (f32[2,128,256]{2,1,0:T(8,128)S(1)}, f32[2,128,256]{2,1,0:T(8,128)S(1)}, u32[]{:S(2)}, u32[]{:S(2)}) collective-permute-start(f32[2,128,256]{2,1,0:T(8,128)S(1)} %get-tuple-element.199), channel_id=1, source_target_pairs={{0,4},{1,5},{2,6},{3,7},{4,0},{5,1},{6,2},{7,3},{8,12},{9,13},{10,... | collective-permute-start | bytes 786440 | tf_op jit(solution)/shard_map/ppermute | solution.py:333
  (57 other events, 443.1 us)
where the time goes:
time: 255 us; the launch traced here: 254 us
  starting transfers between devices  122 us (48%)
  waiting for transfers between devices  77.3 us (30%)
  Pallas kernels  44.9 us (18%)
  local copies, waits for them, and re-layouts  6.74 us (3%)
    ppermute x73, starting transfers between devices, permute(): return lax.ppermute(value, AXES, pairs)  122 us
    ppermute x73, waiting for transfers between devices, permute(): return lax.ppermute(value, AXES, pairs)  77.3 us
    pallas_call x6, Pallas kernels, right_product(): pl.pallas_call(functools.partial(right_kernel, count, chunks), grid=(pair...  16.4 us
    pallas_call x6, Pallas kernels, left_product(): pl.pallas_call(functools.partial(left_kernel, count), grid=(pairs,), in_s...  14.6 us
    unnamed x16, local copies, waits for them, and re-layouts  6.74 us
    pallas_call x6, Pallas kernels, scatter(): pl.pallas_call(functools.partial(scatter_kernel, count, sec_local, chips)...  5.92 us
  transfers between devices with their start and end apart: 73, of which 30 were waited for; matrix products, arithmetic and copies ran while one was open for 1% of the time, Pallas kernels for 11%

commit v1 on v0

v1 whole, which is shorter than its diff:
```python
import functools
import math

import jax
import jax.numpy as jnp
from jax import lax
from jax.experimental import pallas as pl
from jax.experimental.pallas import tpu as pltpu
from jax.sharding import PartitionSpec as P


STEPS = 3
CORES = 2
LANES = 128
AXES = ("sec", "op")
MIB = 1 << 20

VMEM = pl.BlockSpec(memory_space=pltpu.VMEM)
SMEM = pl.BlockSpec(memory_space=pltpu.SMEM)


def params(mib):
    return pltpu.CompilerParams(vmem_limit_bytes=mib * MIB)


def partner_of(place, shift, count):
    if count & (count - 1) == 0:
        return place ^ shift
    return (place + shift) % count


def origin_of(place, shift, count):
    if count & (count - 1) == 0:
        return place ^ shift
    return (place + count - shift) % count


def split(value):
    high = value.astype(jnp.bfloat16)
    low = (value - high.astype(jnp.float32)).astype(jnp.bfloat16)
    return high, low


def widths_of(order):
    if order % (2 * LANES):
        return (order,)
    return (order // 2, order // 2)


def starts_of(widths):
    return [sum(widths[:chunk]) for chunk in range(len(widths))]


def three_pass(left_high, left_low, right_high, right_low):
    dot = functools.partial(jnp.dot, preferred_element_type=jnp.float32)
    return (
        dot(left_high, right_high)
        + dot(left_high, right_low)
        + dot(left_low, right_high)
    )


def prepare_kernel(widths, left, right, left_high, left_low, *rights):
    left_high[0], left_low[0] = split(left[0])
    turned = right[0].T
    for chunk, (start, width) in enumerate(zip(starts_of(widths), widths)):
        part = turned[:, start : start + width]
        rights[2 * chunk][0], rights[2 * chunk + 1][0] = split(part)


def prepare(left_ops, right_ops, widths):
    pairs, order, _ = left_ops.shape

    def spec(width):
        return pl.BlockSpec((1, order, width), lambda p: (p, 0, 0))

    outs = [order] * 2 + [width for width in widths for _ in range(2)]
    high_low = pl.pallas_call(
        functools.partial(prepare_kernel, widths),
        grid=(pairs,),
        in_specs=[spec(order)] * 2,
        out_specs=[spec(width) for width in outs],
        out_shape=[
            jax.ShapeDtypeStruct((pairs, order, width), jnp.bfloat16) for width in outs
        ],
        compiler_params=params(16),
        cost_estimate=pl.CostEstimate(
            flops=4 * pairs * order * order,
            bytes_accessed=16 * pairs * order * order,
            transcendentals=0,
        ),
        name="prepare",
    )(left_ops, right_ops)
    pairs = list(zip(high_low[::2], high_low[1::2]))
    return pairs[0], pairs[1:]


def left_kernel(count, carried, last, start, *refs):
    left_high, left_low, right_high, right_low = refs[:4]
    parts, refs = refs[4 : 4 + count], refs[4 + count :]
    before, refs = refs[:carried], refs[carried:]
    out_high, out_low = refs[:2]
    outs, (high, low, total) = refs[2:-3], refs[-3:]
    place, pair = lax.axis_index("op"), pl.program_id(0)
    rows, width = parts[0].shape

    @pl.when(pair == 0)
    def _():
        for shift in range(count):
            at = pl.ds(pl.multiple_of(origin_of(place, shift, count) * rows, rows), rows)
            high[at, :], low[at, :] = split(parts[shift][...])
        total[...] = before[0][...] if carried else jnp.zeros_like(total)

    product = three_pass(left_high[0], left_low[0], high[...], low[...])
    product_high, product_low = split(product)
    out_high[0], out_low[0] = product_high, product_low
    at = pl.ds(start, width)
    total[...] += three_pass(
        product_high, product_low, right_high[0, at, :], right_low[0, at, :]
    )

    @pl.when(pair == pl.num_programs(0) - 1)
    def _():
        if last:
            put_rows(total, outs, place)
        else:
            outs[0][...] = total[...]


def put_rows(total, outs, place):
    count, rows = len(outs), outs[0].shape[0]
    for shift in range(count):
        start = pl.multiple_of(partner_of(place, shift, count) * rows, rows)
        outs[shift][...] = total[pl.ds(start, rows), :]


def left_product(left, right, parts, before, start, last):
    pairs, order, _ = left[0].shape
    count = len(parts)
    rows, width = parts[0].shape
    first = right[0].shape[2]

    def by_pair(width):
        return pl.BlockSpec((1, order, width), lambda p: (p, 0, 0))

    def whole(rows, width):
        return pl.BlockSpec((rows, width), lambda p: (0, 0))

    out = jax.ShapeDtypeStruct((pairs, order, width), jnp.bfloat16)
    pieces, height = (count, rows) if last else (1, order)
    high, low, *sums = pl.pallas_call(
        functools.partial(left_kernel, count, len(before), last, start),
        grid=(pairs,),
        in_specs=[by_pair(order)] * 2
        + [by_pair(first)] * 2
        + [whole(rows, width)] * count
        + [whole(order, first)] * len(before),
        out_specs=[by_pair(width)] * 2 + [whole(height, first)] * pieces,
        out_shape=[out] * 2
        + [jax.ShapeDtypeStruct((height, first), jnp.float32)] * pieces,
        scratch_shapes=[pltpu.VMEM((order, width), jnp.bfloat16)] * 2
        + [pltpu.VMEM((order, first), jnp.float32)],
        compiler_params=params(16),
        cost_estimate=pl.CostEstimate(
            flops=6 * pairs * order * width * (order + first),
            bytes_accessed=4 * pairs * order * (order + width + first),
            transcendentals=0,
        ),
        name="left_product",
    )(*left, *right, *parts, *before)
    return (high, low), sums


def right_kernel(count, chunks, right_high, right_low, *refs):
    products = refs[: 2 * chunks]
    outs = refs[2 * chunks : 2 * chunks + count]
    total = refs[2 * chunks + count]
    place = lax.axis_index("op")
    pair = pl.program_id(0)
    term, start = 0.0, 0
    for high, low in zip(products[::2], products[1::2]):
        at = pl.ds(start, high.shape[2])
        right = right_high[0, at, :], right_low[0, at, :]
        term = term + three_pass(high[0], low[0], *right)
        start += high.shape[2]

    @pl.when(pair == 0)
    def _():
        total[...] = term

    @pl.when(pair > 0)
    def _():
        total[...] += term

    @pl.when(pair == pl.num_programs(0) - 1)
    def _():
        put_rows(total, outs, place)


def right_product(right, products, count):
    pairs, order, width = right[0].shape
    rows = order // count

    def spec(width):
        return pl.BlockSpec((1, order, width), lambda p: (p, 0, 0))

    out_spec = pl.BlockSpec((rows, width), lambda p: (0, 0))
    return pl.pallas_call(
        functools.partial(right_kernel, count, len(products) // 2),
        grid=(pairs,),
        in_specs=[spec(part.shape[2]) for part in (*right, *products)],
        out_specs=[out_spec] * count,
        out_shape=[jax.ShapeDtypeStruct((rows, width), jnp.float32)] * count,
        scratch_shapes=[pltpu.VMEM((order, width), jnp.float32)],
        compiler_params=params(16),
        cost_estimate=pl.CostEstimate(
            flops=6 * pairs * order * order * width,
            bytes_accessed=4 * pairs * order * (order + width),
            transcendentals=0,
        ),
        name="right_product",
    )(*right, *products)


def scatter_kernel(count, sec_local, chips, own_target, other_target, *refs):
    own, other, outs, home = (
        refs[:count],
        refs[count],
        refs[count + 1 : count + chips],
        refs[count + chips],
    )
    sec, place = lax.axis_index("sec"), lax.axis_index("op")
    chip, core = lax.div(sec, CORES), lax.rem(sec, CORES)
    sign = 1 - 2 * core
    for out in (*outs, home):
        out[...] = jnp.zeros_like(out)
    for shift in range(count):
        block = origin_of(place, shift, count)
        for target, part in (
            (own_target[block], own[shift]),
            (other_target[block], other.at[shift]),
        ):
            target_sec = lax.div(target, sec_local)
            target_chip = lax.div(target_sec, CORES)
            slot = lax.rem(target, CORES * sec_local)
            distance = (target_chip - chip) * sign
            for step in range(1, chips):

                @pl.when(distance == step)
                def _(part=part, slot=slot, out=outs[step - 1]):
                    out[slot] += part[...]

            @pl.when(target_sec == sec)
            def _(part=part, target=target):
                home[lax.rem(target, sec_local)] += part[...]


def scatter(own_target, other_target, own, other, sec_local, chips):
    rows, width = own[0].shape
    count = len(own)
    far = jax.ShapeDtypeStruct((CORES * sec_local, rows, width), jnp.float32)
    home = jax.ShapeDtypeStruct((sec_local, rows, width), jnp.float32)
    *outs, home = pl.pallas_call(
        functools.partial(scatter_kernel, count, sec_local, chips),
        in_specs=[SMEM] * 2 + [VMEM] * (count + 1),
        out_specs=[VMEM] * chips,
        out_shape=[far] * (chips - 1) + [home],
        compiler_params=params(16),
        cost_estimate=pl.CostEstimate(
            flops=2 * count * rows * width,
            bytes_accessed=4 * rows * width * (4 * count + 4 * chips),
            transcendentals=0,
        ),
        name="scatter",
    )(own_target, other_target, *own, other)
    return outs, home


def level_of(chips):
    sec = lax.axis_index("sec")
    chip, core = lax.div(sec, CORES), lax.rem(sec, CORES)
    return jnp.where(core == 0, chip, chips - 1 - chip)


def merge_kernel(chips, near, *refs):
    relayed, same, cross = refs[:-2], refs[-2], refs[-1]
    core = lax.rem(lax.axis_index("sec"), CORES)
    sec_local = same.shape[0]
    relays = level_of(chips) == 1 if relayed else None
    for out, owner in ((same, core), (cross, 1 - core)):
        for sector in range(sec_local):
            at = owner * sec_local + sector
            value = near[at]
            for part in relayed:
                value = value + jnp.where(relays, part[at], 0.0)
            out[sector] = value


def merge(near, relayed, chips):
    sectors, rows, width = near.shape
    half = jax.ShapeDtypeStruct((sectors // CORES, rows, width), jnp.float32)
    return pl.pallas_call(
        functools.partial(merge_kernel, chips),
        in_specs=[VMEM] * (1 + len(relayed)),
        out_specs=[VMEM] * 2,
        out_shape=[half] * 2,
        compiler_params=params(16),
        cost_estimate=pl.CostEstimate(
            flops=near.size, bytes_accessed=12 * near.size, transcendentals=0
        ),
        name="merge",
    )(near, *relayed)


def gather_kernel(chips, home, *refs):
    arrived, send, keep = refs[:-2], refs[-2], refs[-1]
    core = lax.rem(lax.axis_index("sec"), CORES)
    relays = level_of(chips) == 1
    sec_local = home.shape[0]
    for sector in range(sec_local):
        mine = core * sec_local + sector
        theirs = (1 - core) * sec_local + sector
        first = jnp.where(relays, 0.0, arrived[0][theirs])
        second = jnp.where(relays, 0.0, arrived[0][mine])
        for part in arrived[1:]:
            first, second = first + part[theirs], second + part[mine]
        send[sector], keep[sector] = first, home[sector] + second


def gather(home, arrived, chips):
    shape = jax.ShapeDtypeStruct(home.shape, jnp.float32)
    return pl.pallas_call(
        functools.partial(gather_kernel, chips),
        in_specs=[VMEM] * (1 + len(arrived)),
        out_specs=[VMEM] * 2,
        out_shape=[shape] * 2,
        compiler_params=params(16),
        cost_estimate=pl.CostEstimate(
            flops=home.size * 2 * len(arrived),
            bytes_accessed=home.size * 4 * (2 * len(arrived) + 3),
            transcendentals=0,
        ),
        name="gather",
    )(home, *arrived)


def finish(counts, source, summands, before, scale, start, width, send):
    sec_local, rows, _ = summands[0].shape
    count = source.shape[0]
    terms, parts = len(summands), count if send else 0

    def kernel(counts, source, *refs):
        old = refs[terms : len(refs) - 1 - parts]
        new = refs[len(refs) - 1 - parts]
        outs = refs[len(refs) - parts :]
        place = lax.axis_index("op")
        row = place * rows + lax.broadcasted_iota(jnp.int32, (rows, width), 0)
        column = start + lax.broadcasted_iota(jnp.int32, (rows, width), 1)
        for sector in range(sec_local):
            value = None
            for summand in refs[:terms]:
                if summand.shape[2] == width:
                    part = summand[sector]
                else:
                    part = summand[sector, :, start : start + width]
                value = part if value is None else value + part
            live = (row < counts[sector]) & (column < counts[sector])
            value = jnp.where(live, scale * value, 0.0)
            for part in old:
                value = value - part[sector]
            new[sector] = value
        for shift in range(parts):
            outs[shift][...] = new[source[partner_of(place, shift, count)]]

    operands = (*summands, *(() if before is None else (before,)))

    def whole(shape):
        return pl.BlockSpec(shape, lambda i: (0,) * len(shape))

    new = (sec_local, rows, width)
    return pl.pallas_call(
        kernel,
        grid=(1,),
        in_specs=[SMEM] * 2 + [whole(operand.shape) for operand in operands],
        out_specs=[whole(new)] + [whole(new[1:])] * parts,
        out_shape=[jax.ShapeDtypeStruct((sec_local, rows, width), jnp.float32)]
        + [jax.ShapeDtypeStruct((rows, width), jnp.float32)] * parts,
        compiler_params=params(16),
        cost_estimate=pl.CostEstimate(
            flops=4 * sec_local * rows * width,
            bytes_accessed=4 * rows * width * (sec_local * 4 + parts),
            transcendentals=0,
        ),
        name="finish",
    )(counts, source, *operands)


def per_device(shape, theta, counts, source, target, left_ops, right_ops):
    secs, ops = shape["sec"], shape["op"]
    chips = secs // CORES
    sec_local, _, order = theta.shape
    pairs = left_ops.shape[0]
    factor = 0.5 / math.sqrt(target.shape[0] * pairs / sec_local)

    def permute(value, where):
        pairs = []
        for sec in range(secs):
            for op in range(ops):
                to = where(sec, op)
                if to is not None:
                    pairs.append((sec * ops + op, to[0] * ops + to[1]))
        return lax.ppermute(value, AXES, pairs)

    def to_core(value):
        return permute(value, lambda sec, op: (sec ^ 1, op))

    def to_partners(parts):
        here = [parts[0]]
        for shift in range(1, ops):
            here.append(
                permute(
                    parts[shift],
                    lambda sec, op: (sec, partner_of(op, shift, ops)),
                )
            )
        return here

    def along(value, steps, cross=0):
        def where(sec, op):
            chip, core = sec // CORES, sec % CORES
            level = chip if core == 0 else chips - 1 - chip
            if level not in steps or level + steps[level] >= chips:
                return None
            to = chip + (steps[level] if core == 0 else -steps[level])
            return to * CORES + (core ^ cross), op

        return permute(value, where)

    other_target = to_core(target)

    def sums(pieces):
        own = to_partners(pieces)
        other = to_core(jnp.stack(own))
        outs, home = scatter(target, other_target, own, other, sec_local, chips)
        arrived = []
        if chips > 2:
            steps = {level: 2 for level in range(1, chips)} | {0: 1}
            arrived.append(along(outs[1], steps))
        for distance in range(3, chips):
            steps = {level: distance for level in range(chips)}
            arrived.append(along(outs[distance - 1], steps))
        terms = [home]
        if arrived:
            give, keep = gather(home, arrived, chips)
            terms = [keep, to_core(give)]
        if chips > 1:
            halves = merge(outs[0], arrived[:1], chips)
            one = {level: 1 for level in range(chips)}
            for cross, half in enumerate(halves):
                terms.append(along(half, one, cross))
        return terms

    widths = widths_of(order)
    starts = starts_of(widths)
    chunks = range(len(widths))
    before = [None] * len(widths)

    def left_products(parts):
        products, carry = [], []
        for chunk in chunks:
            product, carry = left_product(
                left,
                right[0],
                parts[chunk],
                carry,
                starts[chunk],
                chunk == chunks[-1],
            )
            products.extend(product)
        return products, carry

    now, parts = [], []
    for chunk in chunks:
        new, *send = finish(
            counts,
            source,
            (theta,),
            None,
            1.0,
            starts[chunk],
            widths[chunk],
            True,
        )
        now.append(new)
        parts.append(to_partners(send))
    left, right = prepare(left_ops, right_ops, widths)
    products, first = left_products(parts)

    for step in range(STEPS):
        parts, after = [], []
        for chunk in chunks:
            if chunk == 0:
                pieces = first
            else:
                pieces = right_product(right[chunk], products, ops)
            terms = sums(pieces)
            new, *send = finish(
                counts,
                source,
                terms,
                before[chunk],
                factor if step == 0 else 2.0 * factor,
                starts[chunk],
                widths[chunk],
                step < STEPS - 1,
            )
            after.append(new)
            if send:
                parts.append(to_partners(send))
        before, now = now, after
        if parts:
            products, first = left_products(parts)
    return jnp.concatenate(now, axis=2), jnp.concatenate(before, axis=2)


def solution(mesh):
    in_specs = (
        P("sec", "op", None),
        P("sec"),
        P("sec"),
        P("sec"),
        P(("sec", "op"), None, None),
        P(("sec", "op"), None, None),
    )
    out_specs = (P("sec", "op", None), P("sec", "op", None))
    step = jax.shard_map(
        functools.partial(per_device, dict(mesh.shape)),
        mesh=mesh,
        in_specs=in_specs,
        out_specs=out_specs,
        check_vma=False,
    )

    def solution(theta, *rest):
        return step(theta, *rest)

    return solution
```

time: 255 us -> 237 us (0.929)
  waiting for transfers between devices: 77.3 us -> 31.7 us
  starting transfers between devices: 122 us -> 143 us
  Pallas kernels: 44.9 us -> 50.7 us
    ppermute x73, waiting for transfers between devices: 77.3 us -> 31.7 us  [permute(): return lax.ppermute(value, AXES, pairs)]
    ppermute x73, starting transfers between devices: 122 us -> 143 us  [permute(): return lax.ppermute(value, AXES, pairs)]
    pallas_call x27 -> x30, Pallas kernels: 38.9 us -> 45 us  [the longest x6 28.8 us: left_product(): pl.pallas_call(functools.partial(left_kernel, count, len(before), last, s...]
  transfers between devices with their start and end apart: 73 -> 73, of which waited for: 30 -> 20; matrix products, arithmetic and copies ran while one was open for 1% -> 0% of each run, Pallas kernels for 11% -> 14%
where the time goes in v1:
time: 237 us; the launch traced here: 236 us
  starting transfers between devices  143 us (60%)
  Pallas kernels  50.7 us (21%)
  waiting for transfers between devices  31.7 us (13%)
  local copies, waits for them, and re-layouts  6.74 us (3%)
    ppermute x73, starting transfers between devices, permute(): return lax.ppermute(value, AXES, pairs)  143 us
    ppermute x73, waiting for transfers between devices, permute(): return lax.ppermute(value, AXES, pairs)  31.7 us
    pallas_call x6, Pallas kernels, left_product(): pl.pallas_call(functools.partial(left_kernel, count, len(before), last, s...  28.8 us
    pallas_call x3, Pallas kernels, right_product(): pl.pallas_call(functools.partial(right_kernel, count, len(products) // 2)...  7.69 us
    unnamed x16, local copies, waits for them, and re-layouts  6.74 us
    pallas_call x6, Pallas kernels, scatter(): pl.pallas_call(functools.partial(scatter_kernel, count, sec_local, chips)...  5.74 us
    pallas_call x8, Pallas kernels, finish(): pl.pallas_call(kernel, grid=(1,), in_specs=[SMEM] * 2 + [whole(operand.sh...  5.17 us
  transfers between devices with their start and end apart: 73, of which 20 were waited for; matrix products, arithmetic and copies ran while one was open for 0% of the time, Pallas kernels for 14%

profile of v1, /device:TPU:0, one launch (start us, length us, event | category | flops | bytes accessed | tf_op | source)
XLA Modules:
  0.0 236.1 jit_solution(11985926027218661123)
XLA Ops:
  3.6 3.0 %collective-permute-start.4 = (f32[128,256]{1,0:T(8,128)S(1)}, f32[128,256]{1,0:T(8,128)S(1)}, u32[]{:S(2)}, u32[]{:S(2)}) collective-permute-start(f32[128,256]{1,0:T(8,128)S(1)} %get-tuple-element.136), channel_id=1, source_target_pairs={{0,1},{1,0},{2,3},{3,2},{4,5},{5,4},{6,7},{7,6},{8,9},{9,8},{10,11... | collective-permute-start | bytes 393224 | tf_op jit(solution)/shard_map/ppermute | solution.py:412
  19.0 4.8 %left_product.6 = (bf16[4,512,256]{2,1,0:T(8,128)(2,1)S(1)}, bf16[4,512,256]{2,1,0:T(8,128)(2,1)S(1)}, f32[512,256]{1,0:T(8,128)S(1)}) custom-call(bf16[4,512,512]{2,1,0:T(8,128)(2,1)S(1)} %get-tuple-element.125.refs_0_, bf16[4,512,512]{2,1,0:T(8,128)(2,1)S(1)} %get-tuple-element.126.refs_1_, bf16[4,512,256]{2,1,0:T(8,128)(2,1)S(1)} %get-tuple-element.127.refs_2_, ...), custom_call_target="tpu_custom_call" | custom-call | flops 2415919104 | bytes 8388608 | tf_op jit(solution)/shard_map/left_product/pallas_call | solution.py:151
  24.9 4.8 %left_product.7 = (bf16[4,512,256]{2,1,0:T(8,128)(2,1)S(1)}, bf16[4,512,256]{2,1,0:T(8,128)(2,1)S(1)}, f32[128,256]{1,0:T(8,128)S(1)}, f32[128,256]{1,0:T(8,128)...) custom-call(bf16[4,512,512]{2,1,0:T(8,128)(2,1)S(1)} %get-tuple-element.125.refs_0_, ...), custom_call_target="tpu_custom_call" | custom-call | flops 2415919104 | bytes 8388608 | tf_op jit(solution)/shard_map/left_product/pallas_call | solution.py:151
  47.2 3.5 %collective-permute-start.11 = (f32[4,128,256]{2,1,0:T(8,128)S(1)}, f32[4,128,256]{2,1,0:T(8,128)S(1)}, u32[]{:S(2)}, u32[]{:S(2)}) collective-permute-start(f32[4,128,256]{2,1,0:T(8,128)S(1)} %get-tuple-element.145), channel_id=1, source_target_pairs={{0,8},{1,9},{2,10},{3,11},{8,24},{9,25},{10,26},{11,27},{20,4},{21... | collective-permute-start | bytes 1572872 | tf_op jit(solution)/shard_map/ppermute | solution.py:412
  50.7 3.3 %collective-permute-start.12 = (f32[4,128,256]{2,1,0:T(8,128)S(1)}, f32[4,128,256]{2,1,0:T(8,128)S(1)}, u32[]{:S(2)}, u32[]{:S(2)}) collective-permute-start(f32[4,128,256]{2,1,0:T(8,128)S(1)} %get-tuple-element.146), channel_id=1, source_target_pairs={{0,24},{1,25},{2,26},{3,27},{28,4},{29,5},{30,6},{31,7}} | collective-permute-start | bytes 1572872 | tf_op jit(solution)/shard_map/ppermute | solution.py:412
  58.2 9.3 %collective-permute-start.14 = (f32[2,128,256]{2,1,0:T(8,128)S(1)}, f32[2,128,256]{2,1,0:T(8,128)S(1)}, u32[]{:S(2)}, u32[]{:S(2)}) collective-permute-start(f32[2,128,256]{2,1,0:T(8,128)S(1)} %get-tuple-element.150), channel_id=1, source_target_pairs={{0,8},{1,9},{2,10},{3,11},{8,16},{9,17},{10,18},{11,19},{12,4},{13... | collective-permute-start | bytes 786440 | tf_op jit(solution)/shard_map/ppermute | solution.py:412
  69.7 9.0 %collective-permute-start.26 = (f32[2,128,256]{2,1,0:T(8,128)S(1)}, f32[2,128,256]{2,1,0:T(8,128)S(1)}, u32[]{:S(2)}, u32[]{:S(2)}) collective-permute-start(f32[2,128,256]{2,1,0:T(8,128)S(1)} %get-tuple-element.172), channel_id=1, source_target_pairs={{0,8},{1,9},{2,10},{3,11},{8,16},{9,17},{10,18},{11,19},{12,4},{13... | collective-permute-start | bytes 786440 | tf_op jit(solution)/shard_map/ppermute | solution.py:412
  90.9 4.8 %left_product.8 = (bf16[4,512,256]{2,1,0:T(8,128)(2,1)S(1)}, bf16[4,512,256]{2,1,0:T(8,128)(2,1)S(1)}, f32[512,256]{1,0:T(8,128)S(1)}) custom-call(bf16[4,512,512]{2,1,0:T(8,128)(2,1)S(1)} %get-tuple-element.125.refs_0_, bf16[4,512,512]{2,1,0:T(8,128)(2,1)S(1)} %get-tuple-element.126.refs_1_, bf16[4,512,256]{2,1,0:T(8,128)(2,1)S(1)} %get-tuple-element.127.refs_2_, ...), custom_call_target="tpu_custom_call" | custom-call | flops 2415919104 | bytes 8388608 | tf_op jit(solution)/shard_map/left_product/pallas_call | solution.py:151
  96.3 4.8 %left_product.9 = (bf16[4,512,256]{2,1,0:T(8,128)(2,1)S(1)}, bf16[4,512,256]{2,1,0:T(8,128)(2,1)S(1)}, f32[128,256]{1,0:T(8,128)S(1)}, f32[128,256]{1,0:T(8,128)...) custom-call(bf16[4,512,512]{2,1,0:T(8,128)(2,1)S(1)} %get-tuple-element.125.refs_0_, ...), custom_call_target="tpu_custom_call" | custom-call | flops 2415919104 | bytes 8388608 | tf_op jit(solution)/shard_map/left_product/pallas_call | solution.py:151
  116.8 3.6 %collective-permute-start.47 = (f32[4,128,256]{2,1,0:T(8,128)S(1)}, f32[4,128,256]{2,1,0:T(8,128)S(1)}, u32[]{:S(2)}, u32[]{:S(2)}) collective-permute-start(f32[4,128,256]{2,1,0:T(8,128)S(1)} %get-tuple-element.203), channel_id=1, source_target_pairs={{0,8},{1,9},{2,10},{3,11},{8,24},{9,25},{10,26},{11,27},{20,4},{21... | collective-permute-start | bytes 1572872 | tf_op jit(solution)/shard_map/ppermute | solution.py:412
  120.4 4.5 %collective-permute-start.48 = (f32[4,128,256]{2,1,0:T(8,128)S(1)}, f32[4,128,256]{2,1,0:T(8,128)S(1)}, u32[]{:S(2)}, u32[]{:S(2)}) collective-permute-start(f32[4,128,256]{2,1,0:T(8,128)S(1)} %get-tuple-element.204), channel_id=1, source_target_pairs={{0,24},{1,25},{2,26},{3,27},{28,4},{29,5},{30,6},{31,7}} | collective-permute-start | bytes 1572872 | tf_op jit(solution)/shard_map/ppermute | solution.py:412
  129.2 9.1 %collective-permute-start.50 = (f32[2,128,256]{2,1,0:T(8,128)S(1)}, f32[2,128,256]{2,1,0:T(8,128)S(1)}, u32[]{:S(2)}, u32[]{:S(2)}) collective-permute-start(f32[2,128,256]{2,1,0:T(8,128)S(1)} %get-tuple-element.208), channel_id=1, source_target_pairs={{0,8},{1,9},{2,10},{3,11},{8,16},{9,17},{10,18},{11,19},{12,4},{13... | collective-permute-start | bytes 786440 | tf_op jit(solution)/shard_map/ppermute | solution.py:412
  140.5 9.0 %collective-permute-start.38 = (f32[2,128,256]{2,1,0:T(8,128)S(1)}, f32[2,128,256]{2,1,0:T(8,128)S(1)}, u32[]{:S(2)}, u32[]{:S(2)}) collective-permute-start(f32[2,128,256]{2,1,0:T(8,128)S(1)} %get-tuple-element.191), channel_id=1, source_target_pairs={{0,8},{1,9},{2,10},{3,11},{8,16},{9,17},{10,18},{11,19},{12,4},{13... | collective-permute-start | bytes 786440 | tf_op jit(solution)/shard_map/ppermute | solution.py:412
  162.1 4.8 %left_product.10 = (bf16[4,512,256]{2,1,0:T(8,128)(2,1)S(1)}, bf16[4,512,256]{2,1,0:T(8,128)(2,1)S(1)}, f32[512,256]{1,0:T(8,128)S(1)}) custom-call(bf16[4,512,512]{2,1,0:T(8,128)(2,1)S(1)} %get-tuple-element.125.refs_0_, bf16[4,512,512]{2,1,0:T(8,128)(2,1)S(1)} %get-tuple-element.126.refs_1_, bf16[4,512,256]{2,1,0:T(8,128)(2,1)S(1)} %get-tuple-element.127.refs_2_, ...), custom_call_target="tpu_custom_call" | custom-call | flops 2415919104 | bytes 8388608 | tf_op jit(solution)/shard_map/left_product/pallas_call | solution.py:151
  167.3 4.8 %left_product.11 = (bf16[4,512,256]{2,1,0:T(8,128)(2,1)S(1)}, bf16[4,512,256]{2,1,0:T(8,128)(2,1)S(1)}, f32[128,256]{1,0:T(8,128)S(1)}, f32[128,256]{1,0:T(8,128...) custom-call(bf16[4,512,512]{2,1,0:T(8,128)(2,1)S(1)} %get-tuple-element.125.refs_0_, ...), custom_call_target="tpu_custom_call" | custom-call | flops 2415919104 | bytes 8388608 | tf_op jit(solution)/shard_map/left_product/pallas_call | solution.py:151
  172.1 2.6 %right_product.5 = (f32[128,256]{1,0:T(8,128)S(1)}, f32[128,256]{1,0:T(8,128)S(1)}, f32[128,256]{1,0:T(8,128)S(1)}, f32[128,256]{1,0:T(8,128)S(1)}) custom-call(bf16[4,512,256]{2,1,0:T(8,128)(2,1)S(1)} %get-tuple-element.129.right_high, bf16[4,512,256]{2,1,0:T(8,128)(2,1)S(1)} %get-tuple-element.130.right_low, ...), custom_call_target="tpu_custom_call" | custom-call | flops 1610612736 | bytes 6291456 | tf_op jit(solution)/shard_map/right_product/pallas_call | solution.py:208
  180.7 2.8 %collective-permute-done.65.refs_2_ = f32[128,256]{1,0:T(8,128)S(1)} collective-permute-done((f32[128,256]{1,0:T(8,128)S(1)}, f32[128,256]{1,0:T(8,128)S(1)}, u32[]{:S(2)}, u32[]{:S(2)}) %collective-permute-start.65) | collective-permute-done | bytes 131104 | tf_op jit(solution)/shard_map/ppermute | solution.py:412
  187.2 2.9 %collective-permute-done.55.refs_1_ = f32[128,256]{1,0:T(8,128)S(1)} collective-permute-done((f32[128,256]{1,0:T(8,128)S(1)}, f32[128,256]{1,0:T(8,128)S(1)}, u32[]{:S(2)}, u32[]{:S(2)}) %collective-permute-start.55) | collective-permute-done | bytes 131104 | tf_op jit(solution)/shard_map/ppermute | solution.py:412
  190.1 3.0 %collective-permute-done.56.refs_2_ = f32[128,256]{1,0:T(8,128)S(1)} collective-permute-done((f32[128,256]{1,0:T(8,128)S(1)}, f32[128,256]{1,0:T(8,128)S(1)}, u32[]{:S(2)}, u32[]{:S(2)}) %collective-permute-start.56) | collective-permute-done | bytes 131104 | tf_op jit(solution)/shard_map/ppermute | solution.py:412
  194.2 3.5 %collective-permute-start.68 = (f32[4,128,256]{2,1,0:T(8,128)S(1)}, f32[4,128,256]{2,1,0:T(8,128)S(1)}, u32[]{:S(2)}, u32[]{:S(2)}) collective-permute-start(f32[4,128,256]{2,1,0:T(8,128)S(1)} %get-tuple-element.238), channel_id=1, source_target_pairs={{0,8},{1,9},{2,10},{3,11},{8,24},{9,25},{10,26},{11,27},{20,4},{21... | collective-permute-start | bytes 1572872 | tf_op jit(solution)/shard_map/ppermute | solution.py:412
  197.7 4.2 %collective-permute-start.69 = (f32[4,128,256]{2,1,0:T(8,128)S(1)}, f32[4,128,256]{2,1,0:T(8,128)S(1)}, u32[]{:S(2)}, u32[]{:S(2)}) collective-permute-start(f32[4,128,256]{2,1,0:T(8,128)S(1)} %get-tuple-element.239), channel_id=1, source_target_pairs={{0,24},{1,25},{2,26},{3,27},{28,4},{29,5},{30,6},{31,7}} | collective-permute-start | bytes 1572872 | tf_op jit(solution)/shard_map/ppermute | solution.py:412
  206.1 9.3 %collective-permute-start.71 = (f32[2,128,256]{2,1,0:T(8,128)S(1)}, f32[2,128,256]{2,1,0:T(8,128)S(1)}, u32[]{:S(2)}, u32[]{:S(2)}) collective-permute-start(f32[2,128,256]{2,1,0:T(8,128)S(1)} %get-tuple-element.243), channel_id=1, source_target_pairs={{0,8},{1,9},{2,10},{3,11},{8,16},{9,17},{10,18},{11,19},{12,4},{13... | collective-permute-start | bytes 786440 | tf_op jit(solution)/shard_map/ppermute | solution.py:412
  217.6 9.0 %collective-permute-start.62 = (f32[2,128,256]{2,1,0:T(8,128)S(1)}, f32[2,128,256]{2,1,0:T(8,128)S(1)}, u32[]{:S(2)}, u32[]{:S(2)}) collective-permute-start(f32[2,128,256]{2,1,0:T(8,128)S(1)} %get-tuple-element.226), channel_id=1, source_target_pairs={{0,8},{1,9},{2,10},{3,11},{8,16},{9,17},{10,18},{11,19},{12,4},{13... | collective-permute-start | bytes 786440 | tf_op jit(solution)/shard_map/ppermute | solution.py:412
  230.6 4.0 %collective-permute-done.63.refs_3_ = f32[2,128,256]{2,1,0:T(8,128)S(1)} collective-permute-done((f32[2,128,256]{2,1,0:T(8,128)S(1)}, f32[2,128,256]{2,1,0:T(8,128)S(1)}, u32[]{:S(2)}, u32[]{:S(2)}) %collective-permute-start.63) | collective-permute-done | bytes 262176 | tf_op jit(solution)/shard_map/ppermute | solution.py:412
  (182 shorter events, 110.1 us)
Async XLA Ops:
  3.6 15.3 %collective-permute-start.4 = (f32[128,256]{1,0:T(8,128)S(1)}, f32[128,256]{1,0:T(8,128)S(1)}, u32[]{:S(2)}, u32[]{:S(2)}) collective-permute-start(f32[128,256]{1,0:T(8,128)S(1)} %get-tuple-element.136), channel_id=1, source_target_pairs={{0,1},{1,0},{2,3},{3,2},{4,5},{5,4},{6,7},{7,6},{8,9},{9,8},{10,11... | collective-permute-start | bytes 393224 | tf_op jit(solution)/shard_map/ppermute | solution.py:412
  6.6 12.4 %collective-permute-start.5 = (f32[128,256]{1,0:T(8,128)S(1)}, f32[128,256]{1,0:T(8,128)S(1)}, u32[]{:S(2)}, u32[]{:S(2)}) collective-permute-start(f32[128,256]{1,0:T(8,128)S(1)} %get-tuple-element.137), channel_id=1, source_target_pairs={{0,2},{1,3},{2,0},{3,1},{4,6},{5,7},{6,4},{7,5},{8,10},{9,11},{10,... | collective-permute-start | bytes 393224 | tf_op jit(solution)/shard_map/ppermute | solution.py:412
  8.8 15.1 %collective-permute-start.1 = (f32[128,256]{1,0:T(8,128)S(1)}, f32[128,256]{1,0:T(8,128)S(1)}, u32[]{:S(2)}, u32[]{:S(2)}) collective-permute-start(f32[128,256]{1,0:T(8,128)S(1)} %get-tuple-element.132), channel_id=1, source_target_pairs={{0,1},{1,0},{2,3},{3,2},{4,5},{5,4},{6,7},{7,6},{8,9},{9,8},{10,11... | collective-permute-start | bytes 393224 | tf_op jit(solution)/shard_map/ppermute | solution.py:412
  10.8 13.1 %collective-permute-start.2 = (f32[128,256]{1,0:T(8,128)S(1)}, f32[128,256]{1,0:T(8,128)S(1)}, u32[]{:S(2)}, u32[]{:S(2)}) collective-permute-start(f32[128,256]{1,0:T(8,128)S(1)} %get-tuple-element.133), channel_id=1, source_target_pairs={{0,2},{1,3},{2,0},{3,1},{4,6},{5,7},{6,4},{7,5},{8,10},{9,11},{10,... | collective-permute-start | bytes 393224 | tf_op jit(solution)/shard_map/ppermute | solution.py:412
  50.7 18.8 %collective-permute-start.12 = (f32[4,128,256]{2,1,0:T(8,128)S(1)}, f32[4,128,256]{2,1,0:T(8,128)S(1)}, u32[]{:S(2)}, u32[]{:S(2)}) collective-permute-start(f32[4,128,256]{2,1,0:T(8,128)S(1)} %get-tuple-element.146), channel_id=1, source_target_pairs={{0,24},{1,25},{2,26},{3,27},{28,4},{29,5},{30,6},{31,7}} | collective-permute-start | bytes 1572872 | tf_op jit(solution)/shard_map/ppermute | solution.py:412
  55.0 14.7 %collective-permute-start.23 = (f32[4,128,256]{2,1,0:T(8,128)S(1)}, f32[4,128,256]{2,1,0:T(8,128)S(1)}, u32[]{:S(2)}, u32[]{:S(2)}) collective-permute-start(f32[4,128,256]{2,1,0:T(8,128)S(1)} %get-tuple-element.167), channel_id=1, source_target_pairs={{0,8},{1,9},{2,10},{3,11},{8,24},{9,25},{10,26},{11,27},{20,4},{21... | collective-permute-start | bytes 1572872 | tf_op jit(solution)/shard_map/ppermute | solution.py:412
  56.8 22.0 %collective-permute-start.24 = (f32[4,128,256]{2,1,0:T(8,128)S(1)}, f32[4,128,256]{2,1,0:T(8,128)S(1)}, u32[]{:S(2)}, u32[]{:S(2)}) collective-permute-start(f32[4,128,256]{2,1,0:T(8,128)S(1)} %get-tuple-element.168), channel_id=1, source_target_pairs={{0,24},{1,25},{2,26},{3,27},{28,4},{29,5},{30,6},{31,7}} | collective-permute-start | bytes 1572872 | tf_op jit(solution)/shard_map/ppermute | solution.py:412
  58.2 22.6 %collective-permute-start.14 = (f32[2,128,256]{2,1,0:T(8,128)S(1)}, f32[2,128,256]{2,1,0:T(8,128)S(1)}, u32[]{:S(2)}, u32[]{:S(2)}) collective-permute-start(f32[2,128,256]{2,1,0:T(8,128)S(1)} %get-tuple-element.150), channel_id=1, source_target_pairs={{0,8},{1,9},{2,10},{3,11},{8,16},{9,17},{10,18},{11,19},{12,4},{13... | collective-permute-start | bytes 786440 | tf_op jit(solution)/shard_map/ppermute | solution.py:412
  67.5 13.4 %collective-permute-start.15 = (f32[2,128,256]{2,1,0:T(8,128)S(1)}, f32[2,128,256]{2,1,0:T(8,128)S(1)}, u32[]{:S(2)}, u32[]{:S(2)}) collective-permute-start(f32[2,128,256]{2,1,0:T(8,128)S(1)} %get-tuple-element.151), channel_id=1, source_target_pairs={{0,12},{1,13},{2,14},{3,15},{8,20},{9,21},{10,22},{11,23},{12,0},{... | collective-permute-start | bytes 786440 | tf_op jit(solution)/shard_map/ppermute | solution.py:412
  69.7 13.5 %collective-permute-start.26 = (f32[2,128,256]{2,1,0:T(8,128)S(1)}, f32[2,128,256]{2,1,0:T(8,128)S(1)}, u32[]{:S(2)}, u32[]{:S(2)}) collective-permute-start(f32[2,128,256]{2,1,0:T(8,128)S(1)} %get-tuple-element.172), channel_id=1, source_target_pairs={{0,8},{1,9},{2,10},{3,11},{8,16},{9,17},{10,18},{11,19},{12,4},{13... | collective-permute-start | bytes 786440 | tf_op jit(solution)/shard_map/ppermute | solution.py:412
  116.8 12.3 %collective-permute-start.47 = (f32[4,128,256]{2,1,0:T(8,128)S(1)}, f32[4,128,256]{2,1,0:T(8,128)S(1)}, u32[]{:S(2)}, u32[]{:S(2)}) collective-permute-start(f32[4,128,256]{2,1,0:T(8,128)S(1)} %get-tuple-element.203), channel_id=1, source_target_pairs={{0,8},{1,9},{2,10},{3,11},{8,24},{9,25},{10,26},{11,27},{20,4},{21... | collective-permute-start | bytes 1572872 | tf_op jit(solution)/shard_map/ppermute | solution.py:412
  120.4 19.8 %collective-permute-start.48 = (f32[4,128,256]{2,1,0:T(8,128)S(1)}, f32[4,128,256]{2,1,0:T(8,128)S(1)}, u32[]{:S(2)}, u32[]{:S(2)}) collective-permute-start(f32[4,128,256]{2,1,0:T(8,128)S(1)} %get-tuple-element.204), channel_id=1, source_target_pairs={{0,24},{1,25},{2,26},{3,27},{28,4},{29,5},{30,6},{31,7}} | collective-permute-start | bytes 1572872 | tf_op jit(solution)/shard_map/ppermute | solution.py:412
  125.9 14.5 %collective-permute-start.35 = (f32[4,128,256]{2,1,0:T(8,128)S(1)}, f32[4,128,256]{2,1,0:T(8,128)S(1)}, u32[]{:S(2)}, u32[]{:S(2)}) collective-permute-start(f32[4,128,256]{2,1,0:T(8,128)S(1)} %get-tuple-element.186), channel_id=1, source_target_pairs={{0,8},{1,9},{2,10},{3,11},{8,24},{9,25},{10,26},{11,27},{20,4},{21... | collective-permute-start | bytes 1572872 | tf_op jit(solution)/shard_map/ppermute | solution.py:412
  127.8 21.8 %collective-permute-start.36 = (f32[4,128,256]{2,1,0:T(8,128)S(1)}, f32[4,128,256]{2,1,0:T(8,128)S(1)}, u32[]{:S(2)}, u32[]{:S(2)}) collective-permute-start(f32[4,128,256]{2,1,0:T(8,128)S(1)} %get-tuple-element.187), channel_id=1, source_target_pairs={{0,24},{1,25},{2,26},{3,27},{28,4},{29,5},{30,6},{31,7}} | collective-permute-start | bytes 1572872 | tf_op jit(solution)/shard_map/ppermute | solution.py:412
  129.2 22.4 %collective-permute-start.50 = (f32[2,128,256]{2,1,0:T(8,128)S(1)}, f32[2,128,256]{2,1,0:T(8,128)S(1)}, u32[]{:S(2)}, u32[]{:S(2)}) collective-permute-start(f32[2,128,256]{2,1,0:T(8,128)S(1)} %get-tuple-element.208), channel_id=1, source_target_pairs={{0,8},{1,9},{2,10},{3,11},{8,16},{9,17},{10,18},{11,19},{12,4},{13... | collective-permute-start | bytes 786440 | tf_op jit(solution)/shard_map/ppermute | solution.py:412
  138.3 13.4 %collective-permute-start.51 = (f32[2,128,256]{2,1,0:T(8,128)S(1)}, f32[2,128,256]{2,1,0:T(8,128)S(1)}, u32[]{:S(2)}, u32[]{:S(2)}) collective-permute-start(f32[2,128,256]{2,1,0:T(8,128)S(1)} %get-tuple-element.209), channel_id=1, source_target_pairs={{0,12},{1,13},{2,14},{3,15},{8,20},{9,21},{10,22},{11,23},{12,0},{... | collective-permute-start | bytes 786440 | tf_op jit(solution)/shard_map/ppermute | solution.py:412
  140.5 13.8 %collective-permute-start.38 = (f32[2,128,256]{2,1,0:T(8,128)S(1)}, f32[2,128,256]{2,1,0:T(8,128)S(1)}, u32[]{:S(2)}, u32[]{:S(2)}) collective-permute-start(f32[2,128,256]{2,1,0:T(8,128)S(1)} %get-tuple-element.191), channel_id=1, source_target_pairs={{0,8},{1,9},{2,10},{3,11},{8,16},{9,17},{10,18},{11,19},{12,4},{13... | collective-permute-start | bytes 786440 | tf_op jit(solution)/shard_map/ppermute | solution.py:412
  197.7 19.7 %collective-permute-start.69 = (f32[4,128,256]{2,1,0:T(8,128)S(1)}, f32[4,128,256]{2,1,0:T(8,128)S(1)}, u32[]{:S(2)}, u32[]{:S(2)}) collective-permute-start(f32[4,128,256]{2,1,0:T(8,128)S(1)} %get-tuple-element.239), channel_id=1, source_target_pairs={{0,24},{1,25},{2,26},{3,27},{28,4},{29,5},{30,6},{31,7}} | collective-permute-start | bytes 1572872 | tf_op jit(solution)/shard_map/ppermute | solution.py:412
  202.9 14.7 %collective-permute-start.59 = (f32[4,128,256]{2,1,0:T(8,128)S(1)}, f32[4,128,256]{2,1,0:T(8,128)S(1)}, u32[]{:S(2)}, u32[]{:S(2)}) collective-permute-start(f32[4,128,256]{2,1,0:T(8,128)S(1)} %get-tuple-element.221), channel_id=1, source_target_pairs={{0,8},{1,9},{2,10},{3,11},{8,24},{9,25},{10,26},{11,27},{20,4},{21... | collective-permute-start | bytes 1572872 | tf_op jit(solution)/shard_map/ppermute | solution.py:412
  204.7 22.0 %collective-permute-start.60 = (f32[4,128,256]{2,1,0:T(8,128)S(1)}, f32[4,128,256]{2,1,0:T(8,128)S(1)}, u32[]{:S(2)}, u32[]{:S(2)}) collective-permute-start(f32[4,128,256]{2,1,0:T(8,128)S(1)} %get-tuple-element.222), channel_id=1, source_target_pairs={{0,24},{1,25},{2,26},{3,27},{28,4},{29,5},{30,6},{31,7}} | collective-permute-start | bytes 1572872 | tf_op jit(solution)/shard_map/ppermute | solution.py:412
  206.1 22.6 %collective-permute-start.71 = (f32[2,128,256]{2,1,0:T(8,128)S(1)}, f32[2,128,256]{2,1,0:T(8,128)S(1)}, u32[]{:S(2)}, u32[]{:S(2)}) collective-permute-start(f32[2,128,256]{2,1,0:T(8,128)S(1)} %get-tuple-element.243), channel_id=1, source_target_pairs={{0,8},{1,9},{2,10},{3,11},{8,16},{9,17},{10,18},{11,19},{12,4},{13... | collective-permute-start | bytes 786440 | tf_op jit(solution)/shard_map/ppermute | solution.py:412
  215.4 14.3 %collective-permute-start.72 = (f32[2,128,256]{2,1,0:T(8,128)S(1)}, f32[2,128,256]{2,1,0:T(8,128)S(1)}, u32[]{:S(2)}, u32[]{:S(2)}) collective-permute-start(f32[2,128,256]{2,1,0:T(8,128)S(1)} %get-tuple-element.244), channel_id=1, source_target_pairs={{0,12},{1,13},{2,14},{3,15},{8,20},{9,21},{10,22},{11,23},{12,0},{... | collective-permute-start | bytes 786440 | tf_op jit(solution)/shard_map/ppermute | solution.py:412
  217.5 12.2 %collective-permute-start.70 = (f32[2,128,256]{2,1,0:T(8,128)S(1)}, f32[2,128,256]{2,1,0:T(8,128)S(1)}, u32[]{:S(2)}, u32[]{:S(2)}) collective-permute-start(f32[2,128,256]{2,1,0:T(8,128)S(1)} %get-tuple-element.241), channel_id=1, source_target_pairs={{0,4},{1,5},{2,6},{3,7},{4,0},{5,1},{6,2},{7,3},{8,12},{9,13},{10,... | collective-permute-start | bytes 786440 | tf_op jit(solution)/shard_map/ppermute | solution.py:412
  217.6 12.9 %collective-permute-start.62 = (f32[2,128,256]{2,1,0:T(8,128)S(1)}, f32[2,128,256]{2,1,0:T(8,128)S(1)}, u32[]{:S(2)}, u32[]{:S(2)}) collective-permute-start(f32[2,128,256]{2,1,0:T(8,128)S(1)} %get-tuple-element.226), channel_id=1, source_target_pairs={{0,8},{1,9},{2,10},{3,11},{8,16},{9,17},{10,18},{11,19},{12,4},{13... | collective-permute-start | bytes 786440 | tf_op jit(solution)/shard_map/ppermute | solution.py:412
  (57 other events, 476.0 us)
